TPU v7x, 512 devices: a whole 4x4x16 slice. The times are simulated.
512 devices in a mesh: fsdp: 16 (over x, y), dp: 32 (over z, core).
Axes of the slice: x: 4, y: 4, z: 16, core: 2. Of those that a mesh axis runs over, the one named last changes fastest.
Arguments:
- tokens: bfloat16 [65536, 4096], P(('fsdp', 'dp')), may hold values from -6 to 6
- master_old: float32 [512, 128, 128], P(('fsdp', 'dp')), may hold values from -0.25 to 0.25
- moment_old: float32 [512, 128, 128], P(('fsdp', 'dp')), may hold values from -6 to 6
- second_old: float32 [512, 128, 128], P(('fsdp', 'dp')), may hold values from 0.01 to 1
- old_cell: int32 [112, 4], P('fsdp'), may hold values from 0 to 31, as said below
- new_cell: int32 [112, 4], P('fsdp'), may hold values from 0 to 31, as said below
- regrown: int32 [112, 4], P('fsdp'), may hold values 0 or 1
- new_rows: int32 [112, 4], replicated, may hold values from 0 to 31, as said below
Outputs:
- hidden: bfloat16 [65536, 14336], P(('fsdp', 'dp'))
- master_new: float32 [512, 128, 128], P(('fsdp', 'dp'))
- moment_new: float32 [512, 128, 128], P(('fsdp', 'dp'))
- second_new: float32 [512, 128, 128], P(('fsdp', 'dp'))
Inputs may be any that keep to these rules, and one draw needn't show every extreme that they name: `old_cell`: within one fsdp index, taking its slots column by column and then by k, the old cells strictly increase; a cell's index // 1 is its holder along dp and index % 1 its place in that holder's buffer. `new_cell`: strictly increasing in the same order; every slot's new cell differs from its old cell by at most 4, and by exactly 4 for some slot of every fsdp index. `new_rows`: the 4 block rows of one block column are distinct.
All inputs are finite; a program needn't handle non-finite values. No bound on the sum of `regrown` on one device may be relied on, other than what follows from the above.
Results may differ from a plain program's by a relative error of at most 0.007.
Values may be sent and summed in bfloat16 or wider, within the bound.
No kernel may reach another device: no remote copies, remote signals or barrier semaphores. Data moves between devices by JAX's collectives and lax.ppermute only.
A program may use at most 128 MiB of HBM per device.

v0:
```python
import jax
import jax.numpy as jnp
from jax import lax
from jax.sharding import PartitionSpec as P


def passed_along(block, axis, distance):
    devices = range(lax.axis_size(axis))
    route = [(i - distance, i) for i in devices if i - distance in devices]
    return lax.ppermute(block, axis, route)


def on_device(tokens, master_old, moment_old, second_old, old_cell, new_cell, regrown, new_rows):
    block_size = master_old.shape[1]
    capacity = master_old.shape[0]
    column_count = old_cell.shape[0]
    nonzero_count = old_cell.shape[1]
    slot_count = column_count * nonzero_count
    axis_width = lax.axis_size("dp")
    cell_count = axis_width * capacity
    farthest = min((cell_count - slot_count + capacity - 1) // capacity, axis_width - 1)
    holder = lax.axis_index("dp")
    old_flat = old_cell.reshape(-1)
    new_flat = new_cell.reshape(-1)
    keep_flag = regrown.reshape(-1) == 0
    my_cells = holder * capacity + jnp.arange(capacity, dtype=jnp.int32)
    matches = new_flat[None, :] == my_cells[:, None]
    present = jnp.any(matches & keep_flag[None, :], axis=1)
    source = jnp.sum(jnp.where(matches, old_flat[None, :], 0), axis=1)
    offset = holder - source // capacity
    slot_place = source % capacity
    candidate = jnp.where(offset > 0, 2 * offset - 1, jnp.where(offset < 0, -2 * offset, 0))
    pick_index = candidate * capacity + slot_place
    own_states = (master_old, moment_old, second_old)
    shift_list = []
    for distance in range(1, farthest + 1):
        shift_list.append(distance)
        shift_list.append(-distance)
    received_list = [own_states]
    for by_value in shift_list:
        received_list.append(
            (
                passed_along(own_states[0].astype(jnp.bfloat16), "dp", by_value).astype(
                    jnp.float32
                ),
                passed_along(own_states[1].astype(jnp.bfloat16), "dp", by_value).astype(
                    jnp.float32
                ),
                passed_along(own_states[2].astype(jnp.bfloat16), "dp", by_value).astype(
                    jnp.float32
                ),
            )
        )

    def settle(member):
        pool = jnp.concatenate([entry[member] for entry in received_list], axis=0)
        chosen = jnp.take(pool, pick_index, axis=0, mode="clip")
        return jnp.where(present[:, None, None], chosen, jnp.float32(0.0))

    master_new = settle(0)
    moment_new = settle(1)
    second_new = settle(2)
    cell_blocks = master_new.astype(jnp.bfloat16)
    group_cells = lax.all_gather(cell_blocks, "dp", axis=0, tiled=True)
    panel = jnp.take(group_cells, new_flat, axis=0).reshape(
        column_count, nonzero_count, block_size, block_size
    )
    token_count = tokens.shape[0]
    token_blocks = tokens.reshape(token_count, tokens.shape[1] // block_size, block_size)
    panel_piece = lax.all_gather(panel, "fsdp", axis=0, tiled=True)
    count = panel_piece.shape[0]
    picked = jnp.take(token_blocks, new_rows.reshape(-1), axis=1)
    picked = picked.reshape(token_count, count, nonzero_count, block_size)
    product = jnp.einsum("tcka,ckab->tcb", picked, panel_piece, preferred_element_type=jnp.float32)
    hidden = product.reshape(token_count, count * block_size).astype(jnp.bfloat16)
    return (hidden, master_new, moment_new, second_new)


def solution(mesh):
    return jax.shard_map(
        on_device,
        mesh=mesh,
        in_specs=(
            P(("fsdp", "dp"), None),
            P(("fsdp", "dp"), None, None),
            P(("fsdp", "dp"), None, None),
            P(("fsdp", "dp"), None, None),
            P("fsdp", None),
            P("fsdp", None),
            P("fsdp", None),
            P(),
        ),
        out_specs=(
            P(("fsdp", "dp"), None),
            P(("fsdp", "dp"), None, None),
            P(("fsdp", "dp"), None, None),
            P(("fsdp", "dp"), None, None),
        ),
        check_vma=False,
    )
```

profile of v0, /device:TPU:1, one launch (start us, length us, event | category | flops | bytes accessed | tf_op | source)
XLA Modules:
  0.0 264.1 jit_solution(16962180668199227297)
XLA Ops:
  7.2 0.0 all-gather.3.cloned.1.call-start
  7.2 0.9 fusion.11
  8.1 4.9 %collective-permute-start = (bf16[1,128,128]{2,1,0:T(8,128)(2,1)S(1)}, bf16[1,128,128]{2,1,0:T(8,128)(2,1)S(1)}, u32[]{:S(2)}, u32[]{:S(2)}) collective-permute-start(bf16[1,128,128]{2,1,0:T(8,128)(2,1)S(1)} %get-tuple-element.61), channel_id=1, source_target_pairs={{0,1},{1,2},{2,3},{3,4},{4,5},{5,6},{6,7},{7,8},{8,9},{9,10},{10,1... | collective-permute-start | bytes 98312 | tf_op jit(solution)/shard_map/ppermute | solution.py:10
  13.1 5.1 %collective-permute-start.1 = (bf16[1,128,128]{2,1,0:T(8,128)(2,1)S(1)}, bf16[1,128,128]{2,1,0:T(8,128)(2,1)S(1)}, u32[]{:S(2)}, u32[]{:S(2)}) collective-permute-start(bf16[1,128,128]{2,1,0:T(8,128)(2,1)S(1)} %get-tuple-element.61), channel_id=1, source_target_pairs={{1,0},{2,1},{3,2},{4,3},{5,4},{6,5},{7,6},{8,7},{9,8},{10,9},{11,1... | collective-permute-start | bytes 98312 | tf_op jit(solution)/shard_map/ppermute | solution.py:10
  18.2 1.3 collective-permute-start.2
  19.5 1.3 collective-permute-start.3
  20.8 5.0 %collective-permute-start.4 = (bf16[1,128,128]{2,1,0:T(8,128)(2,1)S(1)}, bf16[1,128,128]{2,1,0:T(8,128)(2,1)S(1)}, u32[]{:S(2)}, u32[]{:S(2)}) collective-permute-start(bf16[1,128,128]{2,1,0:T(8,128)(2,1)S(1)} %get-tuple-element.61), channel_id=1, source_target_pairs={{0,3},{1,4},{2,5},{3,6},{4,7},{5,8},{6,9},{7,10},{8,11},{9,12},{10... | collective-permute-start | bytes 98312 | tf_op jit(solution)/shard_map/ppermute | solution.py:10
  25.9 1.4 and_reduce_fusion
  27.3 1.3 select_reduce_fusion
  29.3 0.0 collective-permute-done
  29.3 1.3 collective-permute-start.5
  30.6 9.2 %collective-permute-start.6 = (bf16[1,128,128]{2,1,0:T(8,128)(2,1)S(1)}, bf16[1,128,128]{2,1,0:T(8,128)(2,1)S(1)}, u32[]{:S(2)}, u32[]{:S(2)}) collective-permute-start(bf16[1,128,128]{2,1,0:T(8,128)(2,1)S(1)} %get-tuple-element.61), channel_id=1, source_target_pairs={{0,4},{1,5},{2,6},{3,7},{4,8},{5,9},{6,10},{7,11},{8,12},{9,13},{1... | collective-permute-start | bytes 98312 | tf_op jit(solution)/shard_map/ppermute | solution.py:10
  39.8 0.0 collective-permute-done.2
  39.8 1.3 collective-permute-start.7
  41.1 0.0 collective-permute-done.5
  41.2 0.0 collective-permute-done.6
  41.2 4.1 %collective-permute-done.7 = bf16[1,128,128]{2,1,0:T(8,128)(2,1)S(1)} collective-permute-done((bf16[1,128,128]{2,1,0:T(8,128)(2,1)S(1)}, bf16[1,128,128]{2,1,0:T(8,128)(2,1)S(1)}, u32[]{:S(2)}, u32[]{:S(2)}) %collective-permute-start.7) | collective-permute-done | bytes 32800 | tf_op jit(solution)/shard_map/ppermute | solution.py:10
  45.3 1.3 fusion.8
  46.6 0.0 all-gather.3.cloned.1.call-update
  46.6 0.0 all-gather.5.cloned.1.call-start
  46.7 0.8 copy.33
  47.5 0.1 reshape.158
  47.5 0.1 copy.32
  47.7 73.8 %all-gather.3.cloned.1.call-done = bf16[32,128,128]{2,1,0:T(8,128)(2,1)} async-done(((bf16[1,128,128]{2,1,0:T(8,128)(2,1)}), bf16[32,128,128]{2,1,0:T(8,128)(2,1)}) %all-gather.3.cloned.1.call-update) | async-done | bytes 1048592 | tf_op jit(solution)/shard_map/all_gather | solution.py:64
  121.4 1.9 gather_fusion
  123.4 1.1 broadcast_select_fusion
  124.4 0.0 all-gather.5.cloned.1.call-update
  124.5 0.9 fusion.9
  125.4 3.2 %collective-permute-start.16 = (bf16[1,128,128]{2,1,0:T(8,128)(2,1)S(1)}, bf16[1,128,128]{2,1,0:T(8,128)(2,1)S(1)}, u32[]{:S(2)}, u32[]{:S(2)}) collective-permute-start(bf16[1,128,128]{2,1,0:T(8,128)(2,1)S(1)} %get-tuple-element.57), channel_id=1, source_target_pairs={{0,1},{1,2},{2,3},{3,4},{4,5},{5,6},{6,7},{7,8},{8,9},{9,10},{10,1... | collective-permute-start | bytes 98312 | tf_op jit(solution)/shard_map/ppermute | solution.py:10
  128.6 1.9 collective-permute-start.17
  130.5 2.3 collective-permute-start.18
  132.8 1.3 collective-permute-start.19
  134.1 6.0 %collective-permute-start.20 = (bf16[1,128,128]{2,1,0:T(8,128)(2,1)S(1)}, bf16[1,128,128]{2,1,0:T(8,128)(2,1)S(1)}, u32[]{:S(2)}, u32[]{:S(2)}) collective-permute-start(bf16[1,128,128]{2,1,0:T(8,128)(2,1)S(1)} %get-tuple-element.57), channel_id=1, source_target_pairs={{0,3},{1,4},{2,5},{3,6},{4,7},{5,8},{6,9},{7,10},{8,11},{9,12},{10... | collective-permute-start | bytes 98312 | tf_op jit(solution)/shard_map/ppermute | solution.py:10
  140.1 0.8 copy.36
  140.9 0.1 reshape.160
  141.0 0.7 compare_and_fusion
  141.7 0.9 fusion.10
  142.7 1.6 copy.35
  144.3 0.7 copy.37
  145.0 0.1 copy.34
  145.1 13.3 %gather_fusion.1 = bf16[448,128,128]{2,1,0:T(8,128)(2,1)} fusion(bf16[128,32,128]{2,0,1:T(8,128)(2,1)S(1)} %copy.37, s32[1024]{0:T(1024)S(1)} %pad_clamp_fusion), kind=kCustom, calls=%fused_computation.1 | custom fusion | bytes 29361920 | tf_op jit(solution)/shard_map/jit(_take)/gather | solution.py:72
  158.3 0.0 collective-permute-done.16
  158.4 1.3 collective-permute-start.21
  159.7 6.6 %collective-permute-start.22 = (bf16[1,128,128]{2,1,0:T(8,128)(2,1)S(1)}, bf16[1,128,128]{2,1,0:T(8,128)(2,1)S(1)}, u32[]{:S(2)}, u32[]{:S(2)}) collective-permute-start(bf16[1,128,128]{2,1,0:T(8,128)(2,1)S(1)} %get-tuple-element.57), channel_id=1, source_target_pairs={{0,4},{1,5},{2,6},{3,7},{4,8},{5,9},{6,10},{7,11},{8,12},{9,13},{1... | collective-permute-start | bytes 98312 | tf_op jit(solution)/shard_map/ppermute | solution.py:10
  166.3 1.3 collective-permute-start.23
  167.6 2.2 collective-permute-start.8
  169.8 0.0 collective-permute-done.20
  169.8 2.2 collective-permute-start.9
  172.0 0.0 collective-permute-done.21
  172.0 6.4 %collective-permute-start.10 = (bf16[1,128,128]{2,1,0:T(8,128)(2,1)S(1)}, bf16[1,128,128]{2,1,0:T(8,128)(2,1)S(1)}, u32[]{:S(2)}, u32[]{:S(2)}) collective-permute-start(bf16[1,128,128]{2,1,0:T(8,128)(2,1)S(1)} %get-tuple-element.59), channel_id=1, source_target_pairs={{0,2},{1,3},{2,4},{3,5},{4,6},{5,7},{6,8},{7,9},{8,10},{9,11},{10,... | collective-permute-start | bytes 98312 | tf_op jit(solution)/shard_map/ppermute | solution.py:10
  178.5 1.3 collective-permute-start.11
  179.8 6.0 %collective-permute-start.12 = (bf16[1,128,128]{2,1,0:T(8,128)(2,1)S(1)}, bf16[1,128,128]{2,1,0:T(8,128)(2,1)S(1)}, u32[]{:S(2)}, u32[]{:S(2)}) collective-permute-start(bf16[1,128,128]{2,1,0:T(8,128)(2,1)S(1)} %get-tuple-element.59), channel_id=1, source_target_pairs={{0,3},{1,4},{2,5},{3,6},{4,7},{5,8},{6,9},{7,10},{8,11},{9,12},{10... | collective-permute-start | bytes 98312 | tf_op jit(solution)/shard_map/ppermute | solution.py:10
  185.9 0.0 collective-permute-done.8
  185.9 1.3 collective-permute-start.13
  187.2 0.0 collective-permute-done.9
  187.2 8.8 %collective-permute-start.14 = (bf16[1,128,128]{2,1,0:T(8,128)(2,1)S(1)}, bf16[1,128,128]{2,1,0:T(8,128)(2,1)S(1)}, u32[]{:S(2)}, u32[]{:S(2)}) collective-permute-start(bf16[1,128,128]{2,1,0:T(8,128)(2,1)S(1)} %get-tuple-element.59), channel_id=1, source_target_pairs={{0,4},{1,5},{2,6},{3,7},{4,8},{5,9},{6,10},{7,11},{8,12},{9,13},{1... | collective-permute-start | bytes 98312 | tf_op jit(solution)/shard_map/ppermute | solution.py:10
  196.0 0.0 collective-permute-done.10
  196.0 1.3 collective-permute-start.15
  197.5 1.3 dynamic-slice_select_fusion
  198.7 3.3 %collective-permute-done.15 = bf16[1,128,128]{2,1,0:T(8,128)(2,1)S(1)} collective-permute-done((bf16[1,128,128]{2,1,0:T(8,128)(2,1)S(1)}, bf16[1,128,128]{2,1,0:T(8,128)(2,1)S(1)}, u32[]{:S(2)}, u32[]{:S(2)}) %collective-permute-start.15) | collective-permute-done | bytes 32800 | tf_op jit(solution)/shard_map/ppermute | solution.py:10
  202.0 1.3 dynamic-slice_select_fusion.1
  203.3 34.5 %all-gather.5.cloned.1.call-done = bf16[112,4,128,128]{3,2,1,0:T(8,128)(2,1)} async-done(((bf16[7,4,128,128]{3,2,1,0:T(8,128)(2,1)}), bf16[112,4,128,128]{3,2,1,0:T(8,128)(2,1)}) %all-gather.5.cloned.1.call-update) | async-done | bytes 14680080 | tf_op jit(solution)/shard_map/all_gather | solution.py:70
  237.7 13.5 %bitcast_convert_fusion = bf16[112,128,128]{2,1,0:T(8,128)(2,1)} fusion(bf16[112,4,128,128]{3,2,1,0:T(8,128)(2,1)} %all-gather.5.cloned.1.call-done, bf16[128,112,4,128]{3,0,2,1:T(8,128)(2,1)} %bitcast.15, pred[112,4]{1,0:T(8,128)(4,1)S(1)} %copy.34), kind=kOutput, calls=%fused_computation.5 | convolution fusion | flops 1888223232 | bytes 33030592 | tf_op jit(solution)/shard_map/tcka,ckab->tcb/dot_general | solution.py:74
  251.2 6.1 %copy.39 = bf16[128,14336]{1,0:T(8,128)(2,1)} copy(bf16[128,14336]{0,1:T(8,128)(2,1)} %bitcast.17) | data formatting | bytes 7340032
  (40 shorter events, 0.2 us)
Async XLA Ops:
  7.2 114.3 %all-gather.3.cloned.1.call-start = ((), (), s32[]{:S(2)}) async-start(), calls=%async_computation | async-start | bytes 1081344 | tf_op jit(solution)/shard_map/all_gather | solution.py:64
  8.1 21.1 %collective-permute-start = (bf16[1,128,128]{2,1,0:T(8,128)(2,1)S(1)}, bf16[1,128,128]{2,1,0:T(8,128)(2,1)S(1)}, u32[]{:S(2)}, u32[]{:S(2)}) collective-permute-start(bf16[1,128,128]{2,1,0:T(8,128)(2,1)S(1)} %get-tuple-element.61), channel_id=1, source_target_pairs={{0,1},{1,2},{2,3},{3,4},{4,5},{5,6},{6,7},{7,8},{8,9},{9,10},{10,1... | collective-permute-start | bytes 98312 | tf_op jit(solution)/shard_map/ppermute | solution.py:10
  13.1 17.5 %collective-permute-start.1 = (bf16[1,128,128]{2,1,0:T(8,128)(2,1)S(1)}, bf16[1,128,128]{2,1,0:T(8,128)(2,1)S(1)}, u32[]{:S(2)}, u32[]{:S(2)}) collective-permute-start(bf16[1,128,128]{2,1,0:T(8,128)(2,1)S(1)} %get-tuple-element.61), channel_id=1, source_target_pairs={{1,0},{2,1},{3,2},{4,3},{5,4},{6,5},{7,6},{8,7},{9,8},{10,9},{11,1... | collective-permute-start | bytes 98312 | tf_op jit(solution)/shard_map/ppermute | solution.py:10
  18.2 21.5 %collective-permute-start.2 = (bf16[1,128,128]{2,1,0:T(8,128)(2,1)S(1)}, bf16[1,128,128]{2,1,0:T(8,128)(2,1)S(1)}, u32[]{:S(2)}, u32[]{:S(2)}) collective-permute-start(bf16[1,128,128]{2,1,0:T(8,128)(2,1)S(1)} %get-tuple-element.61), channel_id=1, source_target_pairs={{0,2},{1,3},{2,4},{3,5},{4,6},{5,7},{6,8},{7,9},{8,10},{9,11},{10,... | collective-permute-start | bytes 98312 | tf_op jit(solution)/shard_map/ppermute | solution.py:10
  19.5 21.6 %collective-permute-start.3 = (bf16[1,128,128]{2,1,0:T(8,128)(2,1)S(1)}, bf16[1,128,128]{2,1,0:T(8,128)(2,1)S(1)}, u32[]{:S(2)}, u32[]{:S(2)}) collective-permute-start(bf16[1,128,128]{2,1,0:T(8,128)(2,1)S(1)} %get-tuple-element.61), channel_id=1, source_target_pairs={{2,0},{3,1},{4,2},{5,3},{6,4},{7,5},{8,6},{9,7},{10,8},{11,9},{12,... | collective-permute-start | bytes 98312 | tf_op jit(solution)/shard_map/ppermute | solution.py:10
  20.8 20.3 %collective-permute-start.4 = (bf16[1,128,128]{2,1,0:T(8,128)(2,1)S(1)}, bf16[1,128,128]{2,1,0:T(8,128)(2,1)S(1)}, u32[]{:S(2)}, u32[]{:S(2)}) collective-permute-start(bf16[1,128,128]{2,1,0:T(8,128)(2,1)S(1)} %get-tuple-element.61), channel_id=1, source_target_pairs={{0,3},{1,4},{2,5},{3,6},{4,7},{5,8},{6,9},{7,10},{8,11},{9,12},{10... | collective-permute-start | bytes 98312 | tf_op jit(solution)/shard_map/ppermute | solution.py:10
  29.3 11.9 %collective-permute-start.5 = (bf16[1,128,128]{2,1,0:T(8,128)(2,1)S(1)}, bf16[1,128,128]{2,1,0:T(8,128)(2,1)S(1)}, u32[]{:S(2)}, u32[]{:S(2)}) collective-permute-start(bf16[1,128,128]{2,1,0:T(8,128)(2,1)S(1)} %get-tuple-element.61), channel_id=1, source_target_pairs={{3,0},{4,1},{5,2},{6,3},{7,4},{8,5},{9,6},{10,7},{11,8},{12,9},{13... | collective-permute-start | bytes 98312 | tf_op jit(solution)/shard_map/ppermute | solution.py:10
  30.6 10.6 %collective-permute-start.6 = (bf16[1,128,128]{2,1,0:T(8,128)(2,1)S(1)}, bf16[1,128,128]{2,1,0:T(8,128)(2,1)S(1)}, u32[]{:S(2)}, u32[]{:S(2)}) collective-permute-start(bf16[1,128,128]{2,1,0:T(8,128)(2,1)S(1)} %get-tuple-element.61), channel_id=1, source_target_pairs={{0,4},{1,5},{2,6},{3,7},{4,8},{5,9},{6,10},{7,11},{8,12},{9,13},{1... | collective-permute-start | bytes 98312 | tf_op jit(solution)/shard_map/ppermute | solution.py:10
  39.8 5.6 %collective-permute-start.7 = (bf16[1,128,128]{2,1,0:T(8,128)(2,1)S(1)}, bf16[1,128,128]{2,1,0:T(8,128)(2,1)S(1)}, u32[]{:S(2)}, u32[]{:S(2)}) collective-permute-start(bf16[1,128,128]{2,1,0:T(8,128)(2,1)S(1)} %get-tuple-element.61), channel_id=1, source_target_pairs={{4,0},{5,1},{6,2},{7,3},{8,4},{9,5},{10,6},{11,7},{12,8},{13,9},{1... | collective-permute-start | bytes 98312 | tf_op jit(solution)/shard_map/ppermute | solution.py:10
  46.6 191.1 %all-gather.5.cloned.1.call-start = ((), (), s32[]{:S(2)}) async-start(), calls=%async_computation.1 | async-start | bytes 15597568 | tf_op jit(solution)/shard_map/all_gather | solution.py:70
  125.4 32.9 %collective-permute-start.16 = (bf16[1,128,128]{2,1,0:T(8,128)(2,1)S(1)}, bf16[1,128,128]{2,1,0:T(8,128)(2,1)S(1)}, u32[]{:S(2)}, u32[]{:S(2)}) collective-permute-start(bf16[1,128,128]{2,1,0:T(8,128)(2,1)S(1)} %get-tuple-element.57), channel_id=1, source_target_pairs={{0,1},{1,2},{2,3},{3,4},{4,5},{5,6},{6,7},{7,8},{8,9},{9,10},{10,1... | collective-permute-start | bytes 98312 | tf_op jit(solution)/shard_map/ppermute | solution.py:10
  128.6 31.1 %collective-permute-start.17 = (bf16[1,128,128]{2,1,0:T(8,128)(2,1)S(1)}, bf16[1,128,128]{2,1,0:T(8,128)(2,1)S(1)}, u32[]{:S(2)}, u32[]{:S(2)}) collective-permute-start(bf16[1,128,128]{2,1,0:T(8,128)(2,1)S(1)} %get-tuple-element.57), channel_id=1, source_target_pairs={{1,0},{2,1},{3,2},{4,3},{5,4},{6,5},{7,6},{8,7},{9,8},{10,9},{11,1... | collective-permute-start | bytes 98312 | tf_op jit(solution)/shard_map/ppermute | solution.py:10
  130.5 35.8 %collective-permute-start.18 = (bf16[1,128,128]{2,1,0:T(8,128)(2,1)S(1)}, bf16[1,128,128]{2,1,0:T(8,128)(2,1)S(1)}, u32[]{:S(2)}, u32[]{:S(2)}) collective-permute-start(bf16[1,128,128]{2,1,0:T(8,128)(2,1)S(1)} %get-tuple-element.57), channel_id=1, source_target_pairs={{0,2},{1,3},{2,4},{3,5},{4,6},{5,7},{6,8},{7,9},{8,10},{9,11},{10,... | collective-permute-start | bytes 98312 | tf_op jit(solution)/shard_map/ppermute | solution.py:10
  132.8 34.8 %collective-permute-start.19 = (bf16[1,128,128]{2,1,0:T(8,128)(2,1)S(1)}, bf16[1,128,128]{2,1,0:T(8,128)(2,1)S(1)}, u32[]{:S(2)}, u32[]{:S(2)}) collective-permute-start(bf16[1,128,128]{2,1,0:T(8,128)(2,1)S(1)} %get-tuple-element.57), channel_id=1, source_target_pairs={{2,0},{3,1},{4,2},{5,3},{6,4},{7,5},{8,6},{9,7},{10,8},{11,9},{12,... | collective-permute-start | bytes 98312 | tf_op jit(solution)/shard_map/ppermute | solution.py:10
  134.1 35.7 %collective-permute-start.20 = (bf16[1,128,128]{2,1,0:T(8,128)(2,1)S(1)}, bf16[1,128,128]{2,1,0:T(8,128)(2,1)S(1)}, u32[]{:S(2)}, u32[]{:S(2)}) collective-permute-start(bf16[1,128,128]{2,1,0:T(8,128)(2,1)S(1)} %get-tuple-element.57), channel_id=1, source_target_pairs={{0,3},{1,4},{2,5},{3,6},{4,7},{5,8},{6,9},{7,10},{8,11},{9,12},{10... | collective-permute-start | bytes 98312 | tf_op jit(solution)/shard_map/ppermute | solution.py:10
  158.4 13.7 %collective-permute-start.21 = (bf16[1,128,128]{2,1,0:T(8,128)(2,1)S(1)}, bf16[1,128,128]{2,1,0:T(8,128)(2,1)S(1)}, u32[]{:S(2)}, u32[]{:S(2)}) collective-permute-start(bf16[1,128,128]{2,1,0:T(8,128)(2,1)S(1)} %get-tuple-element.57), channel_id=1, source_target_pairs={{3,0},{4,1},{5,2},{6,3},{7,4},{8,5},{9,6},{10,7},{11,8},{12,9},{13... | collective-permute-start | bytes 98312 | tf_op jit(solution)/shard_map/ppermute | solution.py:10
  159.7 18.8 %collective-permute-start.22 = (bf16[1,128,128]{2,1,0:T(8,128)(2,1)S(1)}, bf16[1,128,128]{2,1,0:T(8,128)(2,1)S(1)}, u32[]{:S(2)}, u32[]{:S(2)}) collective-permute-start(bf16[1,128,128]{2,1,0:T(8,128)(2,1)S(1)} %get-tuple-element.57), channel_id=1, source_target_pairs={{0,4},{1,5},{2,6},{3,7},{4,8},{5,9},{6,10},{7,11},{8,12},{9,13},{1... | collective-permute-start | bytes 98312 | tf_op jit(solution)/shard_map/ppermute | solution.py:10
  166.3 13.5 %collective-permute-start.23 = (bf16[1,128,128]{2,1,0:T(8,128)(2,1)S(1)}, bf16[1,128,128]{2,1,0:T(8,128)(2,1)S(1)}, u32[]{:S(2)}, u32[]{:S(2)}) collective-permute-start(bf16[1,128,128]{2,1,0:T(8,128)(2,1)S(1)} %get-tuple-element.57), channel_id=1, source_target_pairs={{4,0},{5,1},{6,2},{7,3},{8,4},{9,5},{10,6},{11,7},{12,8},{13,9},{1... | collective-permute-start | bytes 98312 | tf_op jit(solution)/shard_map/ppermute | solution.py:10
  167.6 18.2 %collective-permute-start.8 = (bf16[1,128,128]{2,1,0:T(8,128)(2,1)S(1)}, bf16[1,128,128]{2,1,0:T(8,128)(2,1)S(1)}, u32[]{:S(2)}, u32[]{:S(2)}) collective-permute-start(bf16[1,128,128]{2,1,0:T(8,128)(2,1)S(1)} %get-tuple-element.59), channel_id=1, source_target_pairs={{0,1},{1,2},{2,3},{3,4},{4,5},{5,6},{6,7},{7,8},{8,9},{9,10},{10,1... | collective-permute-start | bytes 98312 | tf_op jit(solution)/shard_map/ppermute | solution.py:10
  169.8 17.3 %collective-permute-start.9 = (bf16[1,128,128]{2,1,0:T(8,128)(2,1)S(1)}, bf16[1,128,128]{2,1,0:T(8,128)(2,1)S(1)}, u32[]{:S(2)}, u32[]{:S(2)}) collective-permute-start(bf16[1,128,128]{2,1,0:T(8,128)(2,1)S(1)} %get-tuple-element.59), channel_id=1, source_target_pairs={{1,0},{2,1},{3,2},{4,3},{5,4},{6,5},{7,6},{8,7},{9,8},{10,9},{11,1... | collective-permute-start | bytes 98312 | tf_op jit(solution)/shard_map/ppermute | solution.py:10
  172.0 24.0 %collective-permute-start.10 = (bf16[1,128,128]{2,1,0:T(8,128)(2,1)S(1)}, bf16[1,128,128]{2,1,0:T(8,128)(2,1)S(1)}, u32[]{:S(2)}, u32[]{:S(2)}) collective-permute-start(bf16[1,128,128]{2,1,0:T(8,128)(2,1)S(1)} %get-tuple-element.59), channel_id=1, source_target_pairs={{0,2},{1,3},{2,4},{3,5},{4,6},{5,7},{6,8},{7,9},{8,10},{9,11},{10,... | collective-permute-start | bytes 98312 | tf_op jit(solution)/shard_map/ppermute | solution.py:10
  178.5 18.8 %collective-permute-start.11 = (bf16[1,128,128]{2,1,0:T(8,128)(2,1)S(1)}, bf16[1,128,128]{2,1,0:T(8,128)(2,1)S(1)}, u32[]{:S(2)}, u32[]{:S(2)}) collective-permute-start(bf16[1,128,128]{2,1,0:T(8,128)(2,1)S(1)} %get-tuple-element.59), channel_id=1, source_target_pairs={{2,0},{3,1},{4,2},{5,3},{6,4},{7,5},{8,6},{9,7},{10,8},{11,9},{12,... | collective-permute-start | bytes 98312 | tf_op jit(solution)/shard_map/ppermute | solution.py:10
  179.8 17.5 %collective-permute-start.12 = (bf16[1,128,128]{2,1,0:T(8,128)(2,1)S(1)}, bf16[1,128,128]{2,1,0:T(8,128)(2,1)S(1)}, u32[]{:S(2)}, u32[]{:S(2)}) collective-permute-start(bf16[1,128,128]{2,1,0:T(8,128)(2,1)S(1)} %get-tuple-element.59), channel_id=1, source_target_pairs={{0,3},{1,4},{2,5},{3,6},{4,7},{5,8},{6,9},{7,10},{8,11},{9,12},{10... | collective-permute-start | bytes 98312 | tf_op jit(solution)/shard_map/ppermute | solution.py:10
  185.9 11.5 %collective-permute-start.13 = (bf16[1,128,128]{2,1,0:T(8,128)(2,1)S(1)}, bf16[1,128,128]{2,1,0:T(8,128)(2,1)S(1)}, u32[]{:S(2)}, u32[]{:S(2)}) collective-permute-start(bf16[1,128,128]{2,1,0:T(8,128)(2,1)S(1)} %get-tuple-element.59), channel_id=1, source_target_pairs={{3,0},{4,1},{5,2},{6,3},{7,4},{8,5},{9,6},{10,7},{11,8},{12,9},{13... | collective-permute-start | bytes 98312 | tf_op jit(solution)/shard_map/ppermute | solution.py:10
  187.2 10.2 %collective-permute-start.14 = (bf16[1,128,128]{2,1,0:T(8,128)(2,1)S(1)}, bf16[1,128,128]{2,1,0:T(8,128)(2,1)S(1)}, u32[]{:S(2)}, u32[]{:S(2)}) collective-permute-start(bf16[1,128,128]{2,1,0:T(8,128)(2,1)S(1)} %get-tuple-element.59), channel_id=1, source_target_pairs={{0,4},{1,5},{2,6},{3,7},{4,8},{5,9},{6,10},{7,11},{8,12},{9,13},{1... | collective-permute-start | bytes 98312 | tf_op jit(solution)/shard_map/ppermute | solution.py:10
  196.0 6.0 %collective-permute-start.15 = (bf16[1,128,128]{2,1,0:T(8,128)(2,1)S(1)}, bf16[1,128,128]{2,1,0:T(8,128)(2,1)S(1)}, u32[]{:S(2)}, u32[]{:S(2)}) collective-permute-start(bf16[1,128,128]{2,1,0:T(8,128)(2,1)S(1)} %get-tuple-element.59), channel_id=1, source_target_pairs={{4,0},{5,1},{6,2},{7,3},{8,4},{9,5},{10,6},{11,7},{12,8},{13,9},{1... | collective-permute-start | bytes 98312 | tf_op jit(solution)/shard_map/ppermute | solution.py:10
Sparse Core Ops, SparseCore 0:
  46.8 74.6 all-gather.2
  125.1 112.6 all-gather.4
where the time goes:
time: 265 us; the launch traced here: 264 us
  waiting for transfers between devices  116 us (44%)
  starting transfers between devices  82.8 us (31%)
  local copies, waits for them, and re-layouts  25.5 us (10%)
  between operations  15.3 us (6%)
  matrix products  13.5 us (5%)
  other arithmetic  11.3 us (4%)
    ppermute x24, starting transfers between devices, passed_along(): return lax.ppermute(block, axis, route)  82.7 us
    all_gather x1, waiting for transfers between devices, on_device(): group_cells = lax.all_gather(cell_blocks, 'dp', axis=0, tiled=True)  73.8 us
    all_gather x1, waiting for transfers between devices, on_device(): panel_piece = lax.all_gather(panel, 'fsdp', axis=0, tiled=True)  34.5 us
    dot_general x1, matrix products, on_device(): jnp.einsum('tcka,ckab->tcb', picked, panel_piece, preferred_element_type=...  13.5 us
    gather x1, local copies, waits for them, and re-layouts, on_device(): picked = jnp.take(token_blocks, new_rows.reshape(-1), axis=1)  13.3 us
    unnamed x4, local copies, waits for them, and re-layouts  9.25 us
    ppermute x24, waiting for transfers between devices, passed_along(): return lax.ppermute(block, axis, route)  7.47 us
  transfers between devices with their start and end apart: 26, of which 4 were waited for; matrix products, arithmetic and copies ran while one was open for 10% of the time, Pallas kernels for 0%

commit v1 on v0

--- a/solution.py
+++ b/solution.py
@@ -61,7 +61,9 @@
     moment_new = settle(1)
     second_new = settle(2)
     cell_blocks = master_new.astype(jnp.bfloat16)
-    group_cells = lax.all_gather(cell_blocks, "dp", axis=0, tiled=True)
+    group_cells = jnp.concatenate(
+        lax.all_to_all(jnp.stack([cell_blocks] * lax.axis_size("dp")), "dp", 0, 0), axis=0
+    )
     panel = jnp.take(group_cells, new_flat, axis=0).reshape(
         column_count, nonzero_count, block_size, block_size
     )

time: 265 us -> 256 us (0.966)
  waiting for transfers between devices: 116 us -> 95.4 us
  starting transfers between devices: 82.8 us -> 93.6 us
    all_gather x1 -> x0, waiting for transfers between devices: 73.8 us -> none  [on_device(): group_cells = lax.all_gather(cell_blocks, 'dp', axis=0, tiled=True)]
    all_to_all x0 -> x1, waiting for transfers between devices: none -> 54.7 us  [on_device(): lax.all_to_all(jnp.stack([cell_blocks] * lax.axis_size('dp')), 'dp', 0, 0)]
    all_to_all x0 -> x1, starting transfers between devices: none -> 15 us  [on_device(): lax.all_to_all(jnp.stack([cell_blocks] * lax.axis_size('dp')), 'dp', 0, 0)]
    ppermute x24, starting transfers between devices: 82.7 us -> 78.6 us  [passed_along(): return lax.ppermute(block, axis, route)]
where the time goes in v1:
time: 256 us; the launch traced here: 254 us
  waiting for transfers between devices  95.4 us (37%)
  starting transfers between devices  93.6 us (37%)
  local copies, waits for them, and re-layouts  25.5 us (10%)
  between operations  15.3 us (6%)
  matrix products  13.5 us (5%)
  other arithmetic  11.1 us (4%)
    ppermute x24, starting transfers between devices, passed_along(): return lax.ppermute(block, axis, route)  78.6 us
    all_to_all x1, waiting for transfers between devices, on_device(): lax.all_to_all(jnp.stack([cell_blocks] * lax.axis_size('dp')), 'dp', 0, 0)  54.7 us
    all_gather x1, waiting for transfers between devices, on_device(): panel_piece = lax.all_gather(panel, 'fsdp', axis=0, tiled=True)  33.1 us
    all_to_all x1, starting transfers between devices, on_device(): lax.all_to_all(jnp.stack([cell_blocks] * lax.axis_size('dp')), 'dp', 0, 0)  15 us
    dot_general x1, matrix products, on_device(): jnp.einsum('tcka,ckab->tcb', picked, panel_piece, preferred_element_type=...  13.5 us
    gather x1, local copies, waits for them, and re-layouts, on_device(): picked = jnp.take(token_blocks, new_rows.reshape(-1), axis=1)  13.3 us
    unnamed x4, local copies, waits for them, and re-layouts  9.25 us
    ppermute x24, waiting for transfers between devices, passed_along(): return lax.ppermute(block, axis, route)  7.52 us
  transfers between devices with their start and end apart: 26, of which 4 were waited for; matrix products, arithmetic and copies ran while one was open for 10% of the time, Pallas kernels for 0%

profile of v1, /device:TPU:1, one launch (start us, length us, event | category | flops | bytes accessed | tf_op | source)
XLA Modules:
  0.0 254.3 jit_solution(15302428616678011010)
XLA Ops:
  7.2 0.9 fusion.10
  8.1 4.9 %collective-permute-start = (bf16[1,128,128]{2,1,0:T(8,128)(2,1)S(1)}, bf16[1,128,128]{2,1,0:T(8,128)(2,1)S(1)}, u32[]{:S(2)}, u32[]{:S(2)}) collective-permute-start(bf16[1,128,128]{2,1,0:T(8,128)(2,1)S(1)} %get-tuple-element.61), channel_id=1, source_target_pairs={{0,1},{1,2},{2,3},{3,4},{4,5},{5,6},{6,7},{7,8},{8,9},{9,10},{10,1... | collective-permute-start | bytes 98312 | tf_op jit(solution)/shard_map/ppermute | solution.py:10
  13.0 5.1 %collective-permute-start.1 = (bf16[1,128,128]{2,1,0:T(8,128)(2,1)S(1)}, bf16[1,128,128]{2,1,0:T(8,128)(2,1)S(1)}, u32[]{:S(2)}, u32[]{:S(2)}) collective-permute-start(bf16[1,128,128]{2,1,0:T(8,128)(2,1)S(1)} %get-tuple-element.61), channel_id=1, source_target_pairs={{1,0},{2,1},{3,2},{4,3},{5,4},{6,5},{7,6},{8,7},{9,8},{10,9},{11,1... | collective-permute-start | bytes 98312 | tf_op jit(solution)/shard_map/ppermute | solution.py:10
  18.2 1.3 collective-permute-start.2
  19.5 1.3 collective-permute-start.3
  20.8 5.0 %collective-permute-start.4 = (bf16[1,128,128]{2,1,0:T(8,128)(2,1)S(1)}, bf16[1,128,128]{2,1,0:T(8,128)(2,1)S(1)}, u32[]{:S(2)}, u32[]{:S(2)}) collective-permute-start(bf16[1,128,128]{2,1,0:T(8,128)(2,1)S(1)} %get-tuple-element.61), channel_id=1, source_target_pairs={{0,3},{1,4},{2,5},{3,6},{4,7},{5,8},{6,9},{7,10},{8,11},{9,12},{10... | collective-permute-start | bytes 98312 | tf_op jit(solution)/shard_map/ppermute | solution.py:10
  25.8 1.3 and_reduce_fusion
  27.2 1.3 select_reduce_fusion
  29.2 0.0 collective-permute-done
  29.2 1.3 collective-permute-start.5
  30.5 0.0 collective-permute-done.1
  30.5 9.2 %collective-permute-start.6 = (bf16[1,128,128]{2,1,0:T(8,128)(2,1)S(1)}, bf16[1,128,128]{2,1,0:T(8,128)(2,1)S(1)}, u32[]{:S(2)}, u32[]{:S(2)}) collective-permute-start(bf16[1,128,128]{2,1,0:T(8,128)(2,1)S(1)} %get-tuple-element.61), channel_id=1, source_target_pairs={{0,4},{1,5},{2,6},{3,7},{4,8},{5,9},{6,10},{7,11},{8,12},{9,13},{1... | collective-permute-start | bytes 98312 | tf_op jit(solution)/shard_map/ppermute | solution.py:10
  39.7 0.0 collective-permute-done.2
  39.7 1.3 collective-permute-start.7
  41.0 0.0 collective-permute-done.3
  41.1 0.0 collective-permute-done.6
  41.1 4.1 %collective-permute-done.7 = bf16[1,128,128]{2,1,0:T(8,128)(2,1)S(1)} collective-permute-done((bf16[1,128,128]{2,1,0:T(8,128)(2,1)S(1)}, bf16[1,128,128]{2,1,0:T(8,128)(2,1)S(1)}, u32[]{:S(2)}, u32[]{:S(2)}) %collective-permute-start.7) | collective-permute-done | bytes 32800 | tf_op jit(solution)/shard_map/ppermute | solution.py:10
  45.3 1.2 convert_bitcast_fusion
  46.5 1.2 stack.2
  47.7 15.0 %all-to-all-start = ((bf16[32,1,128,128]{3,2,1,0:T(8,128)(2,1)}), bf16[32,1,128,128]{3,2,1,0:T(8,128)(2,1)S(1)}, u32[]{:S(2)}, u32[]{:S(2)}) async-start(bf16[32,1,128,128]{3,2,1,0:T(8,128)(2,1)} %stack.2), calls=%async_computation | async-start | bytes 2097152 | tf_op jit(solution)/shard_map/all_to_all | solution.py:65
  62.6 0.0 all-gather.2.cloned.1.call-start
  62.7 0.8 copy.32
  63.5 0.1 reshape.168
  63.5 0.1 copy.31
  63.7 54.7 %all-to-all-done = bf16[32,1,128,128]{3,2,1,0:T(8,128)(2,1)S(1)} async-done(((bf16[32,1,128,128]{3,2,1,0:T(8,128)(2,1)}), bf16[32,1,128,128]{3,2,1,0:T(8,128)(2,1)S(1)}, u32[]{:S(2)}, u32[]{:S(2)}) %all-to-all-start) | async-done | bytes 1048608 | tf_op jit(solution)/shard_map/all_to_all | solution.py:65
  118.4 0.7 gather_fusion
  119.1 1.1 broadcast_select_fusion
  120.2 0.0 all-gather.2.cloned.1.call-update
  120.2 0.9 fusion.8
  121.1 1.9 collective-permute-start.16
  123.1 2.4 collective-permute-start.17
  125.5 1.5 collective-permute-start.18
  127.0 1.3 collective-permute-start.19
  128.3 5.6 %collective-permute-start.20 = (bf16[1,128,128]{2,1,0:T(8,128)(2,1)S(1)}, bf16[1,128,128]{2,1,0:T(8,128)(2,1)S(1)}, u32[]{:S(2)}, u32[]{:S(2)}) collective-permute-start(bf16[1,128,128]{2,1,0:T(8,128)(2,1)S(1)} %get-tuple-element.57), channel_id=1, source_target_pairs={{0,3},{1,4},{2,5},{3,6},{4,7},{5,8},{6,9},{7,10},{8,11},{9,12},{10... | collective-permute-start | bytes 98312 | tf_op jit(solution)/shard_map/ppermute | solution.py:10
  133.9 0.8 copy.35
  134.7 0.1 reshape.170
  134.8 0.7 compare_and_fusion
  135.5 0.9 fusion.9
  136.5 1.6 copy.34
  138.1 0.7 copy.36
  138.8 0.1 copy.33
  138.9 13.3 %gather_fusion.1 = bf16[448,128,128]{2,1,0:T(8,128)(2,1)} fusion(bf16[128,32,128]{2,0,1:T(8,128)(2,1)S(1)} %copy.36, s32[1024]{0:T(1024)S(1)} %pad_clamp_fusion), kind=kCustom, calls=%fused_computation.1 | custom fusion | bytes 29361920 | tf_op jit(solution)/shard_map/jit(_take)/gather | solution.py:74
  152.2 0.0 collective-permute-done.16
  152.2 1.3 collective-permute-start.21
  153.5 0.0 collective-permute-done.17
  153.5 4.3 %collective-permute-start.22 = (bf16[1,128,128]{2,1,0:T(8,128)(2,1)S(1)}, bf16[1,128,128]{2,1,0:T(8,128)(2,1)S(1)}, u32[]{:S(2)}, u32[]{:S(2)}) collective-permute-start(bf16[1,128,128]{2,1,0:T(8,128)(2,1)S(1)} %get-tuple-element.57), channel_id=1, source_target_pairs={{0,4},{1,5},{2,6},{3,7},{4,8},{5,9},{6,10},{7,11},{8,12},{9,13},{1... | collective-permute-start | bytes 98312 | tf_op jit(solution)/shard_map/ppermute | solution.py:10
  157.8 0.0 collective-permute-done.18
  157.8 1.3 collective-permute-start.23
  159.2 0.0 collective-permute-done.19
  159.2 3.6 %collective-permute-start.8 = (bf16[1,128,128]{2,1,0:T(8,128)(2,1)S(1)}, bf16[1,128,128]{2,1,0:T(8,128)(2,1)S(1)}, u32[]{:S(2)}, u32[]{:S(2)}) collective-permute-start(bf16[1,128,128]{2,1,0:T(8,128)(2,1)S(1)} %get-tuple-element.59), channel_id=1, source_target_pairs={{0,1},{1,2},{2,3},{3,4},{4,5},{5,6},{6,7},{7,8},{8,9},{9,10},{10,1... | collective-permute-start | bytes 98312 | tf_op jit(solution)/shard_map/ppermute | solution.py:10
  162.8 0.0 collective-permute-done.20
  162.8 1.9 collective-permute-start.9
  164.7 5.3 %collective-permute-start.10 = (bf16[1,128,128]{2,1,0:T(8,128)(2,1)S(1)}, bf16[1,128,128]{2,1,0:T(8,128)(2,1)S(1)}, u32[]{:S(2)}, u32[]{:S(2)}) collective-permute-start(bf16[1,128,128]{2,1,0:T(8,128)(2,1)S(1)} %get-tuple-element.59), channel_id=1, source_target_pairs={{0,2},{1,3},{2,4},{3,5},{4,6},{5,7},{6,8},{7,9},{8,10},{9,11},{10,... | collective-permute-start | bytes 98312 | tf_op jit(solution)/shard_map/ppermute | solution.py:10
  170.1 1.3 collective-permute-start.11
  171.4 6.0 %collective-permute-start.12 = (bf16[1,128,128]{2,1,0:T(8,128)(2,1)S(1)}, bf16[1,128,128]{2,1,0:T(8,128)(2,1)S(1)}, u32[]{:S(2)}, u32[]{:S(2)}) collective-permute-start(bf16[1,128,128]{2,1,0:T(8,128)(2,1)S(1)} %get-tuple-element.59), channel_id=1, source_target_pairs={{0,3},{1,4},{2,5},{3,6},{4,7},{5,8},{6,9},{7,10},{8,11},{9,12},{10... | collective-permute-start | bytes 98312 | tf_op jit(solution)/shard_map/ppermute | solution.py:10
  177.4 1.3 collective-permute-start.13
  178.7 8.8 %collective-permute-start.14 = (bf16[1,128,128]{2,1,0:T(8,128)(2,1)S(1)}, bf16[1,128,128]{2,1,0:T(8,128)(2,1)S(1)}, u32[]{:S(2)}, u32[]{:S(2)}) collective-permute-start(bf16[1,128,128]{2,1,0:T(8,128)(2,1)S(1)} %get-tuple-element.59), channel_id=1, source_target_pairs={{0,4},{1,5},{2,6},{3,7},{4,8},{5,9},{6,10},{7,11},{8,12},{9,13},{1... | collective-permute-start | bytes 98312 | tf_op jit(solution)/shard_map/ppermute | solution.py:10
  187.6 1.3 collective-permute-start.15
  189.0 1.2 dynamic-slice_select_fusion
  190.2 3.3 %collective-permute-done.15 = bf16[1,128,128]{2,1,0:T(8,128)(2,1)S(1)} collective-permute-done((bf16[1,128,128]{2,1,0:T(8,128)(2,1)S(1)}, bf16[1,128,128]{2,1,0:T(8,128)(2,1)S(1)}, u32[]{:S(2)}, u32[]{:S(2)}) %collective-permute-start.15) | collective-permute-done | bytes 32800 | tf_op jit(solution)/shard_map/ppermute | solution.py:10
  193.5 1.2 dynamic-slice_select_fusion.1
  194.7 33.1 %all-gather.2.cloned.1.call-done = bf16[112,4,128,128]{3,2,1,0:T(8,128)(2,1)} async-done(((bf16[7,4,128,128]{3,2,1,0:T(8,128)(2,1)}), bf16[112,4,128,128]{3,2,1,0:T(8,128)(2,1)}) %all-gather.2.cloned.1.call-update) | async-done | bytes 14680080 | tf_op jit(solution)/shard_map/all_gather | solution.py:72
  227.9 13.5 %bitcast_convert_fusion = bf16[112,128,128]{2,1,0:T(8,128)(2,1)} fusion(bf16[112,4,128,128]{3,2,1,0:T(8,128)(2,1)} %all-gather.2.cloned.1.call-done, bf16[128,112,4,128]{3,0,2,1:T(8,128)(2,1)} %bitcast.18, pred[112,4]{1,0:T(8,128)(4,1)S(1)} %copy.33), kind=kOutput, calls=%fused_computation.5 | convolution fusion | flops 1888223232 | bytes 33030592 | tf_op jit(solution)/shard_map/tcka,ckab->tcb/dot_general | solution.py:76
  241.3 6.1 %copy.38 = bf16[128,14336]{1,0:T(8,128)(2,1)} copy(bf16[128,14336]{0,1:T(8,128)(2,1)} %bitcast.21) | data formatting | bytes 7340032
  (40 shorter events, 0.2 us)
Async XLA Ops:
  8.1 21.1 %collective-permute-start = (bf16[1,128,128]{2,1,0:T(8,128)(2,1)S(1)}, bf16[1,128,128]{2,1,0:T(8,128)(2,1)S(1)}, u32[]{:S(2)}, u32[]{:S(2)}) collective-permute-start(bf16[1,128,128]{2,1,0:T(8,128)(2,1)S(1)} %get-tuple-element.61), channel_id=1, source_target_pairs={{0,1},{1,2},{2,3},{3,4},{4,5},{5,6},{6,7},{7,8},{8,9},{9,10},{10,1... | collective-permute-start | bytes 98312 | tf_op jit(solution)/shard_map/ppermute | solution.py:10
  13.0 17.4 %collective-permute-start.1 = (bf16[1,128,128]{2,1,0:T(8,128)(2,1)S(1)}, bf16[1,128,128]{2,1,0:T(8,128)(2,1)S(1)}, u32[]{:S(2)}, u32[]{:S(2)}) collective-permute-start(bf16[1,128,128]{2,1,0:T(8,128)(2,1)S(1)} %get-tuple-element.61), channel_id=1, source_target_pairs={{1,0},{2,1},{3,2},{4,3},{5,4},{6,5},{7,6},{8,7},{9,8},{10,9},{11,1... | collective-permute-start | bytes 98312 | tf_op jit(solution)/shard_map/ppermute | solution.py:10
  18.2 21.5 %collective-permute-start.2 = (bf16[1,128,128]{2,1,0:T(8,128)(2,1)S(1)}, bf16[1,128,128]{2,1,0:T(8,128)(2,1)S(1)}, u32[]{:S(2)}, u32[]{:S(2)}) collective-permute-start(bf16[1,128,128]{2,1,0:T(8,128)(2,1)S(1)} %get-tuple-element.61), channel_id=1, source_target_pairs={{0,2},{1,3},{2,4},{3,5},{4,6},{5,7},{6,8},{7,9},{8,10},{9,11},{10,... | collective-permute-start | bytes 98312 | tf_op jit(solution)/shard_map/ppermute | solution.py:10
  19.5 21.5 %collective-permute-start.3 = (bf16[1,128,128]{2,1,0:T(8,128)(2,1)S(1)}, bf16[1,128,128]{2,1,0:T(8,128)(2,1)S(1)}, u32[]{:S(2)}, u32[]{:S(2)}) collective-permute-start(bf16[1,128,128]{2,1,0:T(8,128)(2,1)S(1)} %get-tuple-element.61), channel_id=1, source_target_pairs={{2,0},{3,1},{4,2},{5,3},{6,4},{7,5},{8,6},{9,7},{10,8},{11,9},{12,... | collective-permute-start | bytes 98312 | tf_op jit(solution)/shard_map/ppermute | solution.py:10
  20.8 20.2 %collective-permute-start.4 = (bf16[1,128,128]{2,1,0:T(8,128)(2,1)S(1)}, bf16[1,128,128]{2,1,0:T(8,128)(2,1)S(1)}, u32[]{:S(2)}, u32[]{:S(2)}) collective-permute-start(bf16[1,128,128]{2,1,0:T(8,128)(2,1)S(1)} %get-tuple-element.61), channel_id=1, source_target_pairs={{0,3},{1,4},{2,5},{3,6},{4,7},{5,8},{6,9},{7,10},{8,11},{9,12},{10... | collective-permute-start | bytes 98312 | tf_op jit(solution)/shard_map/ppermute | solution.py:10
  29.2 11.9 %collective-permute-start.5 = (bf16[1,128,128]{2,1,0:T(8,128)(2,1)S(1)}, bf16[1,128,128]{2,1,0:T(8,128)(2,1)S(1)}, u32[]{:S(2)}, u32[]{:S(2)}) collective-permute-start(bf16[1,128,128]{2,1,0:T(8,128)(2,1)S(1)} %get-tuple-element.61), channel_id=1, source_target_pairs={{3,0},{4,1},{5,2},{6,3},{7,4},{8,5},{9,6},{10,7},{11,8},{12,9},{13... | collective-permute-start | bytes 98312 | tf_op jit(solution)/shard_map/ppermute | solution.py:10
  30.5 10.6 %collective-permute-start.6 = (bf16[1,128,128]{2,1,0:T(8,128)(2,1)S(1)}, bf16[1,128,128]{2,1,0:T(8,128)(2,1)S(1)}, u32[]{:S(2)}, u32[]{:S(2)}) collective-permute-start(bf16[1,128,128]{2,1,0:T(8,128)(2,1)S(1)} %get-tuple-element.61), channel_id=1, source_target_pairs={{0,4},{1,5},{2,6},{3,7},{4,8},{5,9},{6,10},{7,11},{8,12},{9,13},{1... | collective-permute-start | bytes 98312 | tf_op jit(solution)/shard_map/ppermute | solution.py:10
  39.7 5.6 %collective-permute-start.7 = (bf16[1,128,128]{2,1,0:T(8,128)(2,1)S(1)}, bf16[1,128,128]{2,1,0:T(8,128)(2,1)S(1)}, u32[]{:S(2)}, u32[]{:S(2)}) collective-permute-start(bf16[1,128,128]{2,1,0:T(8,128)(2,1)S(1)} %get-tuple-element.61), channel_id=1, source_target_pairs={{4,0},{5,1},{6,2},{7,3},{8,4},{9,5},{10,6},{11,7},{12,8},{13,9},{1... | collective-permute-start | bytes 98312 | tf_op jit(solution)/shard_map/ppermute | solution.py:10
  47.7 70.7 %all-to-all-start = ((bf16[32,1,128,128]{3,2,1,0:T(8,128)(2,1)}), bf16[32,1,128,128]{3,2,1,0:T(8,128)(2,1)S(1)}, u32[]{:S(2)}, u32[]{:S(2)}) async-start(bf16[32,1,128,128]{3,2,1,0:T(8,128)(2,1)} %stack.2), calls=%async_computation | async-start | bytes 2097152 | tf_op jit(solution)/shard_map/all_to_all | solution.py:65
  62.6 165.2 %all-gather.2.cloned.1.call-start = ((), (), s32[]{:S(2)}) async-start(), calls=%async_computation.1 | async-start | bytes 15597568 | tf_op jit(solution)/shard_map/all_gather | solution.py:72
  121.1 31.1 %collective-permute-start.16 = (bf16[1,128,128]{2,1,0:T(8,128)(2,1)S(1)}, bf16[1,128,128]{2,1,0:T(8,128)(2,1)S(1)}, u32[]{:S(2)}, u32[]{:S(2)}) collective-permute-start(bf16[1,128,128]{2,1,0:T(8,128)(2,1)S(1)} %get-tuple-element.57), channel_id=1, source_target_pairs={{0,1},{1,2},{2,3},{3,4},{4,5},{5,6},{6,7},{7,8},{8,9},{9,10},{10,1... | collective-permute-start | bytes 98312 | tf_op jit(solution)/shard_map/ppermute | solution.py:10
  123.1 30.4 %collective-permute-start.17 = (bf16[1,128,128]{2,1,0:T(8,128)(2,1)S(1)}, bf16[1,128,128]{2,1,0:T(8,128)(2,1)S(1)}, u32[]{:S(2)}, u32[]{:S(2)}) collective-permute-start(bf16[1,128,128]{2,1,0:T(8,128)(2,1)S(1)} %get-tuple-element.57), channel_id=1, source_target_pairs={{1,0},{2,1},{3,2},{4,3},{5,4},{6,5},{7,6},{8,7},{9,8},{10,9},{11,1... | collective-permute-start | bytes 98312 | tf_op jit(solution)/shard_map/ppermute | solution.py:10
  125.5 32.4 %collective-permute-start.18 = (bf16[1,128,128]{2,1,0:T(8,128)(2,1)S(1)}, bf16[1,128,128]{2,1,0:T(8,128)(2,1)S(1)}, u32[]{:S(2)}, u32[]{:S(2)}) collective-permute-start(bf16[1,128,128]{2,1,0:T(8,128)(2,1)S(1)} %get-tuple-element.57), channel_id=1, source_target_pairs={{0,2},{1,3},{2,4},{3,5},{4,6},{5,7},{6,8},{7,9},{8,10},{9,11},{10,... | collective-permute-start | bytes 98312 | tf_op jit(solution)/shard_map/ppermute | solution.py:10
  127.0 32.2 %collective-permute-start.19 = (bf16[1,128,128]{2,1,0:T(8,128)(2,1)S(1)}, bf16[1,128,128]{2,1,0:T(8,128)(2,1)S(1)}, u32[]{:S(2)}, u32[]{:S(2)}) collective-permute-start(bf16[1,128,128]{2,1,0:T(8,128)(2,1)S(1)} %get-tuple-element.57), channel_id=1, source_target_pairs={{2,0},{3,1},{4,2},{5,3},{6,4},{7,5},{8,6},{9,7},{10,8},{11,9},{12,... | collective-permute-start | bytes 98312 | tf_op jit(solution)/shard_map/ppermute | solution.py:10
  128.3 34.5 %collective-permute-start.20 = (bf16[1,128,128]{2,1,0:T(8,128)(2,1)S(1)}, bf16[1,128,128]{2,1,0:T(8,128)(2,1)S(1)}, u32[]{:S(2)}, u32[]{:S(2)}) collective-permute-start(bf16[1,128,128]{2,1,0:T(8,128)(2,1)S(1)} %get-tuple-element.57), channel_id=1, source_target_pairs={{0,3},{1,4},{2,5},{3,6},{4,7},{5,8},{6,9},{7,10},{8,11},{9,12},{10... | collective-permute-start | bytes 98312 | tf_op jit(solution)/shard_map/ppermute | solution.py:10
  152.2 12.5 %collective-permute-start.21 = (bf16[1,128,128]{2,1,0:T(8,128)(2,1)S(1)}, bf16[1,128,128]{2,1,0:T(8,128)(2,1)S(1)}, u32[]{:S(2)}, u32[]{:S(2)}) collective-permute-start(bf16[1,128,128]{2,1,0:T(8,128)(2,1)S(1)} %get-tuple-element.57), channel_id=1, source_target_pairs={{3,0},{4,1},{5,2},{6,3},{7,4},{8,5},{9,6},{10,7},{11,8},{12,9},{13... | collective-permute-start | bytes 98312 | tf_op jit(solution)/shard_map/ppermute | solution.py:10
  153.5 16.6 %collective-permute-start.22 = (bf16[1,128,128]{2,1,0:T(8,128)(2,1)S(1)}, bf16[1,128,128]{2,1,0:T(8,128)(2,1)S(1)}, u32[]{:S(2)}, u32[]{:S(2)}) collective-permute-start(bf16[1,128,128]{2,1,0:T(8,128)(2,1)S(1)} %get-tuple-element.57), channel_id=1, source_target_pairs={{0,4},{1,5},{2,6},{3,7},{4,8},{5,9},{6,10},{7,11},{8,12},{9,13},{1... | collective-permute-start | bytes 98312 | tf_op jit(solution)/shard_map/ppermute | solution.py:10
  157.8 13.5 %collective-permute-start.23 = (bf16[1,128,128]{2,1,0:T(8,128)(2,1)S(1)}, bf16[1,128,128]{2,1,0:T(8,128)(2,1)S(1)}, u32[]{:S(2)}, u32[]{:S(2)}) collective-permute-start(bf16[1,128,128]{2,1,0:T(8,128)(2,1)S(1)} %get-tuple-element.57), channel_id=1, source_target_pairs={{4,0},{5,1},{6,2},{7,3},{8,4},{9,5},{10,6},{11,7},{12,8},{13,9},{1... | collective-permute-start | bytes 98312 | tf_op jit(solution)/shard_map/ppermute | solution.py:10
  159.2 18.2 %collective-permute-start.8 = (bf16[1,128,128]{2,1,0:T(8,128)(2,1)S(1)}, bf16[1,128,128]{2,1,0:T(8,128)(2,1)S(1)}, u32[]{:S(2)}, u32[]{:S(2)}) collective-permute-start(bf16[1,128,128]{2,1,0:T(8,128)(2,1)S(1)} %get-tuple-element.59), channel_id=1, source_target_pairs={{0,1},{1,2},{2,3},{3,4},{4,5},{5,6},{6,7},{7,8},{8,9},{9,10},{10,1... | collective-permute-start | bytes 98312 | tf_op jit(solution)/shard_map/ppermute | solution.py:10
  162.8 16.0 %collective-permute-start.9 = (bf16[1,128,128]{2,1,0:T(8,128)(2,1)S(1)}, bf16[1,128,128]{2,1,0:T(8,128)(2,1)S(1)}, u32[]{:S(2)}, u32[]{:S(2)}) collective-permute-start(bf16[1,128,128]{2,1,0:T(8,128)(2,1)S(1)} %get-tuple-element.59), channel_id=1, source_target_pairs={{1,0},{2,1},{3,2},{4,3},{5,4},{6,5},{7,6},{8,7},{9,8},{10,9},{11,1... | collective-permute-start | bytes 98312 | tf_op jit(solution)/shard_map/ppermute | solution.py:10
  164.7 22.8 %collective-permute-start.10 = (bf16[1,128,128]{2,1,0:T(8,128)(2,1)S(1)}, bf16[1,128,128]{2,1,0:T(8,128)(2,1)S(1)}, u32[]{:S(2)}, u32[]{:S(2)}) collective-permute-start(bf16[1,128,128]{2,1,0:T(8,128)(2,1)S(1)} %get-tuple-element.59), channel_id=1, source_target_pairs={{0,2},{1,3},{2,4},{3,5},{4,6},{5,7},{6,8},{7,9},{8,10},{9,11},{10,... | collective-permute-start | bytes 98312 | tf_op jit(solution)/shard_map/ppermute | solution.py:10
  170.1 18.8 %collective-permute-start.11 = (bf16[1,128,128]{2,1,0:T(8,128)(2,1)S(1)}, bf16[1,128,128]{2,1,0:T(8,128)(2,1)S(1)}, u32[]{:S(2)}, u32[]{:S(2)}) collective-permute-start(bf16[1,128,128]{2,1,0:T(8,128)(2,1)S(1)} %get-tuple-element.59), channel_id=1, source_target_pairs={{2,0},{3,1},{4,2},{5,3},{6,4},{7,5},{8,6},{9,7},{10,8},{11,9},{12,... | collective-permute-start | bytes 98312 | tf_op jit(solution)/shard_map/ppermute | solution.py:10
  171.4 17.5 %collective-permute-start.12 = (bf16[1,128,128]{2,1,0:T(8,128)(2,1)S(1)}, bf16[1,128,128]{2,1,0:T(8,128)(2,1)S(1)}, u32[]{:S(2)}, u32[]{:S(2)}) collective-permute-start(bf16[1,128,128]{2,1,0:T(8,128)(2,1)S(1)} %get-tuple-element.59), channel_id=1, source_target_pairs={{0,3},{1,4},{2,5},{3,6},{4,7},{5,8},{6,9},{7,10},{8,11},{9,12},{10... | collective-permute-start | bytes 98312 | tf_op jit(solution)/shard_map/ppermute | solution.py:10
  177.4 11.5 %collective-permute-start.13 = (bf16[1,128,128]{2,1,0:T(8,128)(2,1)S(1)}, bf16[1,128,128]{2,1,0:T(8,128)(2,1)S(1)}, u32[]{:S(2)}, u32[]{:S(2)}) collective-permute-start(bf16[1,128,128]{2,1,0:T(8,128)(2,1)S(1)} %get-tuple-element.59), channel_id=1, source_target_pairs={{3,0},{4,1},{5,2},{6,3},{7,4},{8,5},{9,6},{10,7},{11,8},{12,9},{13... | collective-permute-start | bytes 98312 | tf_op jit(solution)/shard_map/ppermute | solution.py:10
  178.7 10.2 %collective-permute-start.14 = (bf16[1,128,128]{2,1,0:T(8,128)(2,1)S(1)}, bf16[1,128,128]{2,1,0:T(8,128)(2,1)S(1)}, u32[]{:S(2)}, u32[]{:S(2)}) collective-permute-start(bf16[1,128,128]{2,1,0:T(8,128)(2,1)S(1)} %get-tuple-element.59), channel_id=1, source_target_pairs={{0,4},{1,5},{2,6},{3,7},{4,8},{5,9},{6,10},{7,11},{8,12},{9,13},{1... | collective-permute-start | bytes 98312 | tf_op jit(solution)/shard_map/ppermute | solution.py:10
  187.6 6.0 %collective-permute-start.15 = (bf16[1,128,128]{2,1,0:T(8,128)(2,1)S(1)}, bf16[1,128,128]{2,1,0:T(8,128)(2,1)S(1)}, u32[]{:S(2)}, u32[]{:S(2)}) collective-permute-start(bf16[1,128,128]{2,1,0:T(8,128)(2,1)S(1)} %get-tuple-element.59), channel_id=1, source_target_pairs={{4,0},{5,1},{6,2},{7,3},{8,4},{9,5},{10,6},{11,7},{12,8},{13,9},{1... | collective-permute-start | bytes 98312 | tf_op jit(solution)/shard_map/ppermute | solution.py:10
Sparse Core Ops, SparseCore 0:
  120.3 107.5 all-gather.1
